TPU v7x, 512 devices: a whole 4x4x16 slice. The times are simulated.
512 devices in a mesh: dp: 16 (over x_hi, y, core), factor: 32 (over x_lo, z).
Axes of the slice: x: 4 (x_hi: 2, x_lo: 2; x = x_hi * 2 + x_lo), y: 4, z: 16, core: 2. Of those that a mesh axis runs over, the one named last changes fastest.
Arguments:
- activations: bfloat16 [2048, 8192], P('dp', 'factor'), may hold values from -12 to 12
- gradients: bfloat16 [2048, 8192], P('dp', 'factor'), may hold values from -12 to 12
- act_basis: bfloat16 [8192, 8192], P('dp', 'factor'), may hold values from -0.0625 to 0.0625
- grad_basis: bfloat16 [8192, 8192], P('dp', 'factor'), may hold values from -0.0625 to 0.0625
Outputs:
- corrected: float32 [8192, 8192], P('factor', 'dp')
All inputs are finite; a program needn't handle non-finite values.
Results may differ from a plain program's by a relative error of at most 0.00062.
Values may be sent and summed in bfloat16 or wider, within the bound.
No kernel may reach another device: no remote copies, remote signals or barrier semaphores. Data moves between devices by JAX's collectives and lax.ppermute only.
A program may use at most 64 MiB of HBM per device.

v0:
```python
import jax
import jax.numpy as jnp
from jax import lax
from jax.sharding import PartitionSpec as P


def on_device(activations, gradients, act_basis, grad_basis):
    act_full, grad_full = (
        lax.all_gather(activations, "factor", axis=1, tiled=True),
        lax.all_gather(gradients, "factor", axis=1, tiled=True),
    )
    columns = act_full
    rotated_act = jnp.dot(
        columns,
        lax.all_gather(act_basis, "dp", axis=0, tiled=True),
        preferred_element_type=jnp.float32,
    )
    columns = grad_full
    rotated_grad = jnp.dot(
        columns,
        lax.all_gather(grad_basis, "dp", axis=0, tiled=True),
        preferred_element_type=jnp.float32,
    )
    act_square = (rotated_act * rotated_act).astype(jnp.bfloat16)
    grad_square = (rotated_grad * rotated_grad).astype(jnp.bfloat16)
    act_every = lax.all_gather(act_square, "dp", axis=0, tiled=True)
    grad_wide = lax.all_gather(grad_square, "factor", axis=1, tiled=True)
    grad_block = lax.all_to_all(grad_wide, "dp", split_axis=1, concat_axis=0, tiled=True)
    total = lax.dot_general(
        act_every, grad_block, (((0,), (0,)), ((), ())), preferred_element_type=jnp.float32
    )
    return total * (1.0 / act_every.shape[0])


def solution(mesh):
    return jax.shard_map(
        on_device,
        mesh=mesh,
        in_specs=(P("dp", "factor"), P("dp", "factor"), P("dp", "factor"), P("dp", "factor")),
        out_specs=P("factor", "dp"),
        check_vma=False,
    )
```

profile of v0, /device:TPU:1, one launch (start us, length us, event | category | flops | bytes accessed | tf_op | source)
XLA Modules:
  0.0 617.3 jit_solution(8077619885345062295)
XLA Ops:
  6.5 0.0 all-gather.13.cloned.1.call-start
  6.5 0.7 all-gather.13.cloned.1.call-update
  7.3 0.0 all-gather.15.cloned.1.call-start
  7.3 0.7 all-gather.15.cloned.1.call-update
  8.0 0.0 all-gather.7.cloned.1.call-start
  8.1 0.7 all-gather.7.cloned.1.call-update
  8.7 0.0 all-gather.9.cloned.1.call-start
  8.8 0.5 all-gather.9.cloned.1.call-update
  9.3 0.0 all-gather.17.cloned.1.call-start
  9.4 111.3 %all-gather.13.cloned.1.call-done = bf16[128,8192]{1,0:T(8,128)(2,1)} async-done(((bf16[128,256]{1,0:T(8,128)(2,1)}), bf16[128,8192]{1,0:T(8,128)(2,1)}) %all-gather.13.cloned.1.call-update) | async-done | bytes 2097168 | tf_op jit(solution)/shard_map/all_gather | solution.py:10
  120.7 92.8 %all-gather.15.cloned.1.call-done = bf16[8192,256]{1,0:T(8,128)(2,1)} async-done(((bf16[512,256]{1,0:T(8,128)(2,1)}), bf16[8192,256]{1,0:T(8,128)(2,1)}) %all-gather.15.cloned.1.call-update) | async-done | bytes 4194320 | tf_op jit(solution)/shard_map/all_gather | solution.py:21
  213.5 4.2 fusion.1
  217.6 0.0 all-gather.17.cloned.1.call-update
  217.6 0.0 all-gather.11.cloned.1.call-start
  217.7 101.3 %all-gather.7.cloned.1.call-done = bf16[128,8192]{1,0:T(8,128)(2,1)} async-done(((bf16[128,256]{1,0:T(8,128)(2,1)}), bf16[128,8192]{1,0:T(8,128)(2,1)}) %all-gather.7.cloned.1.call-update) | async-done | bytes 2097168 | tf_op jit(solution)/shard_map/all_gather | solution.py:9
  319.0 92.6 %all-gather.9.cloned.1.call-done = bf16[8192,256]{1,0:T(8,128)(2,1)} async-done(((bf16[512,256]{1,0:T(8,128)(2,1)}), bf16[8192,256]{1,0:T(8,128)(2,1)}) %all-gather.9.cloned.1.call-update) | async-done | bytes 4194320 | tf_op jit(solution)/shard_map/all_gather | solution.py:15
  411.7 4.2 fusion
  415.8 0.0 all-gather.11.cloned.1.call-update
  415.8 101.2 %all-gather.17.cloned.1.call-done = bf16[128,8192]{1,0:T(8,128)(2,1)} async-done(((bf16[128,256]{1,0:T(8,128)(2,1)}), bf16[128,8192]{1,0:T(8,128)(2,1)}) %all-gather.17.cloned.1.call-update) | async-done | bytes 2097168 | tf_op jit(solution)/shard_map/all_gather | solution.py:27
  517.1 3.2 copy.8
  520.2 29.6 %all-to-all-start = ((bf16[128,16,512]{2,0,1:T(8,128)(2,1)}), bf16[128,16,512]{2,0,1:T(8,128)(2,1)S(1)}, u32[]{:S(2)}, u32[]{:S(2)}) async-start(bf16[128,16,512]{2,0,1:T(8,128)(2,1)} %bitcast.12), calls=%async_computation | async-start | bytes 4194304 | tf_op jit(solution)/shard_map/all_to_all | solution.py:28
  549.8 57.8 %all-gather.11.cloned.1.call-done = bf16[2048,256]{1,0:T(8,128)(2,1)} async-done(((bf16[128,256]{1,0:T(8,128)(2,1)}), bf16[2048,256]{1,0:T(8,128)(2,1)}) %all-gather.11.cloned.1.call-update) | async-done | bytes 1048592 | tf_op jit(solution)/shard_map/all_gather | solution.py:26
  607.7 0.0 all-to-all-done
  607.7 2.7 convolution_multiply_fusion
Async XLA Ops:
  6.5 114.2 %all-gather.13.cloned.1.call-start = ((), (), s32[]{:S(2)}) async-start(), calls=%async_computation.4 | async-start | bytes 2162688 | tf_op jit(solution)/shard_map/all_gather | solution.py:10
  7.3 206.2 %all-gather.15.cloned.1.call-start = ((), (), s32[]{:S(2)}) async-start(), calls=%async_computation.5 | async-start | bytes 4456448 | tf_op jit(solution)/shard_map/all_gather | solution.py:21
  8.0 311.0 %all-gather.7.cloned.1.call-start = ((), (), s32[]{:S(2)}) async-start(), calls=%async_computation.1 | async-start | bytes 2162688 | tf_op jit(solution)/shard_map/all_gather | solution.py:9
  8.7 402.9 %all-gather.9.cloned.1.call-start = ((), (), s32[]{:S(2)}) async-start(), calls=%async_computation.2 | async-start | bytes 4456448 | tf_op jit(solution)/shard_map/all_gather | solution.py:15
  9.3 507.7 %all-gather.17.cloned.1.call-start = ((), (), s32[]{:S(2)}) async-start(), calls=%async_computation.6 | async-start | bytes 2162688 | tf_op jit(solution)/shard_map/all_gather | solution.py:27
  217.6 390.0 %all-gather.11.cloned.1.call-start = ((), (), s32[]{:S(2)}) async-start(), calls=%async_computation.3 | async-start | bytes 1114112 | tf_op jit(solution)/shard_map/all_gather | solution.py:26
  520.2 87.5 %all-to-all-start = ((bf16[128,16,512]{2,0,1:T(8,128)(2,1)}), bf16[128,16,512]{2,0,1:T(8,128)(2,1)S(1)}, u32[]{:S(2)}, u32[]{:S(2)}) async-start(bf16[128,16,512]{2,0,1:T(8,128)(2,1)} %bitcast.12), calls=%async_computation | async-start | bytes 4194304 | tf_op jit(solution)/shard_map/all_to_all | solution.py:28
Sparse Core Ops, SparseCore 0:
  9.4 111.2 all-gather.12
  124.0 89.3 all-gather.14
  215.5 103.5 all-gather.6
  322.2 89.3 all-gather.8
  413.5 103.5 all-gather.16
  520.3 87.3 all-gather.10
where the time goes:
time: 617 us
  waiting for transfers between devices  560 us (91%)
  starting transfers between devices  29.8 us (5%)
  between operations  13.5 us (2%)
  matrix products  11.1 us (2%)
    all_gather x1, waiting for transfers between devices, on_device(): lax.all_gather(gradients, 'factor', axis=1, tiled=True)  111 us
    all_gather x1, waiting for transfers between devices, on_device(): lax.all_gather(activations, 'factor', axis=1, tiled=True)  101 us
    all_gather x1, waiting for transfers between devices, on_device(): grad_wide = lax.all_gather(grad_square, 'factor', axis=1, tiled=True)  101 us
    all_gather x1, waiting for transfers between devices, on_device(): lax.all_gather(grad_basis, 'dp', axis=0, tiled=True)  92.8 us
    all_gather x1, waiting for transfers between devices, on_device(): lax.all_gather(act_basis, 'dp', axis=0, tiled=True)  92.6 us
    all_gather x1, waiting for transfers between devices, on_device(): act_every = lax.all_gather(act_square, 'dp', axis=0, tiled=True)  57.8 us
    all_to_all x1, starting transfers between devices, on_device(): lax.all_to_all(grad_wide, 'dp', split_axis=1, concat_axis=0, tiled=True)  29.6 us
  transfers between devices with their start and end apart: 7, of which 6 were waited for; matrix products, arithmetic and copies ran while one was open for 2% of the time, Pallas kernels for 0%

commit v1 on v0

--- a/solution.py
+++ b/solution.py
@@ -23,7 +23,10 @@
     )
     act_square = (rotated_act * rotated_act).astype(jnp.bfloat16)
     grad_square = (rotated_grad * rotated_grad).astype(jnp.bfloat16)
-    act_every = lax.all_gather(act_square, "dp", axis=0, tiled=True)
+    count = lax.axis_size("dp")
+    shards = jnp.stack([act_square for _ in range(count)])
+    shards = lax.all_to_all(shards, "dp", split_axis=0, concat_axis=0)
+    act_every = jnp.concatenate(shards, axis=0)
     grad_wide = lax.all_gather(grad_square, "factor", axis=1, tiled=True)
     grad_block = lax.all_to_all(grad_wide, "dp", split_axis=1, concat_axis=0, tiled=True)
     total = lax.dot_general(

time: 617 us -> 585 us (0.948)
  waiting for transfers between devices: 560 us -> 497 us
  blocking collectives: 0 us -> 57 us
  starting transfers between devices: 29.8 us -> 3.84 us
    all_gather x1 -> x0, waiting for transfers between devices: 57.8 us -> none  [on_device(): act_every = lax.all_gather(act_square, 'dp', axis=0, tiled=True)]
    all_to_all x0 -> x1, blocking collectives: none -> 57 us  [on_device(): lax.all_to_all(grad_wide, 'dp', split_axis=1, concat_axis=0, tiled=True)]
    all_to_all x1, starting transfers between devices: 29.6 us -> 3.69 us  [on_device(): shards = lax.all_to_all(shards, 'dp', split_axis=0, concat_axis=0)]
  transfers between devices with their start and end apart: 7 -> 6, of which waited for: 6 -> 5; matrix products, arithmetic and copies ran while one was open for 2% -> 2% of each run, Pallas kernels for 0% -> 0%
where the time goes in v1:
time: 585 us; the launch traced here: 584 us
  waiting for transfers between devices  497 us (85%)
  blocking collectives  57 us (10%)
  between operations  13.2 us (2%)
  matrix products  10.2 us (2%)
    all_gather x1, waiting for transfers between devices, on_device(): lax.all_gather(gradients, 'factor', axis=1, tiled=True)  111 us
    all_gather x1, waiting for transfers between devices, on_device(): lax.all_gather(activations, 'factor', axis=1, tiled=True)  101 us
    all_gather x1, waiting for transfers between devices, on_device(): grad_wide = lax.all_gather(grad_square, 'factor', axis=1, tiled=True)  96.5 us
    all_gather x1, waiting for transfers between devices, on_device(): lax.all_gather(grad_basis, 'dp', axis=0, tiled=True)  92.8 us
    all_gather x1, waiting for transfers between devices, on_device(): lax.all_gather(act_basis, 'dp', axis=0, tiled=True)  92.6 us
    all_to_all x1, blocking collectives, on_device(): lax.all_to_all(grad_wide, 'dp', split_axis=1, concat_axis=0, tiled=True)  57 us
  transfers between devices with their start and end apart: 6, of which 5 were waited for; matrix products, arithmetic and copies ran while one was open for 2% of the time, Pallas kernels for 0%

profile of v1, /device:TPU:1, one launch (start us, length us, event | category | flops | bytes accessed | tf_op | source)
XLA Modules:
  0.0 584.4 jit_solution(3107935663304719954)
XLA Ops:
  6.5 0.0 all-gather.10.cloned.1.call-start
  6.5 0.7 all-gather.10.cloned.1.call-update
  7.3 0.0 all-gather.12.cloned.1.call-start
  7.3 0.7 all-gather.12.cloned.1.call-update
  8.0 0.0 all-gather.6.cloned.1.call-start
  8.1 0.7 all-gather.6.cloned.1.call-update
  8.7 0.0 all-gather.8.cloned.1.call-start
  8.8 0.5 all-gather.8.cloned.1.call-update
  9.3 0.0 all-gather.14.cloned.1.call-start
  9.4 111.3 %all-gather.10.cloned.1.call-done = bf16[128,8192]{1,0:T(8,128)(2,1)} async-done(((bf16[128,256]{1,0:T(8,128)(2,1)}), bf16[128,8192]{1,0:T(8,128)(2,1)}) %all-gather.10.cloned.1.call-update) | async-done | bytes 2097168 | tf_op jit(solution)/shard_map/all_gather | solution.py:10
  120.7 92.8 %all-gather.12.cloned.1.call-done = bf16[8192,256]{1,0:T(8,128)(2,1)} async-done(((bf16[512,256]{1,0:T(8,128)(2,1)}), bf16[8192,256]{1,0:T(8,128)(2,1)}) %all-gather.12.cloned.1.call-update) | async-done | bytes 4194320 | tf_op jit(solution)/shard_map/all_gather | solution.py:21
  213.5 4.2 fusion.9
  217.6 0.0 all-gather.14.cloned.1.call-update
  217.7 101.4 %all-gather.6.cloned.1.call-done = bf16[128,8192]{1,0:T(8,128)(2,1)} async-done(((bf16[128,256]{1,0:T(8,128)(2,1)}), bf16[128,8192]{1,0:T(8,128)(2,1)}) %all-gather.6.cloned.1.call-update) | async-done | bytes 2097168 | tf_op jit(solution)/shard_map/all_gather | solution.py:9
  319.0 92.6 %all-gather.8.cloned.1.call-done = bf16[8192,256]{1,0:T(8,128)(2,1)} async-done(((bf16[512,256]{1,0:T(8,128)(2,1)}), bf16[8192,256]{1,0:T(8,128)(2,1)}) %all-gather.8.cloned.1.call-update) | async-done | bytes 4194320 | tf_op jit(solution)/shard_map/all_gather | solution.py:15
  411.7 4.6 fusion.8
  416.2 1.2 stack.2
  417.4 3.7 all-to-all-start
  421.1 96.5 %all-gather.14.cloned.1.call-done = bf16[128,8192]{1,0:T(8,128)(2,1)} async-done(((bf16[128,256]{1,0:T(8,128)(2,1)}), bf16[128,8192]{1,0:T(8,128)(2,1)}) %all-gather.14.cloned.1.call-update) | async-done | bytes 2097168 | tf_op jit(solution)/shard_map/all_gather | solution.py:30
  517.6 1.8 copy.8
  519.4 0.0 all-to-all-done
  519.4 57.0 %all_to_all.21 = bf16[128,16,512]{2,0,1:T(8,128)(2,1)S(1)} all-to-all(bf16[128,16,512]{2,0,1:T(8,128)(2,1)S(1)} %bitcast.20), channel_id=1, replica_groups=mesh['dp'=16,'factor'=32] {'dp'}, dimensions={1} | all-to-all | bytes 4194304 | tf_op jit(solution)/shard_map/all_to_all | solution.py:31
  576.3 1.5 fusion.5
Async XLA Ops:
  6.5 114.2 %all-gather.10.cloned.1.call-start = ((), (), s32[]{:S(2)}) async-start(), calls=%async_computation.4 | async-start | bytes 2162688 | tf_op jit(solution)/shard_map/all_gather | solution.py:10
  7.3 206.2 %all-gather.12.cloned.1.call-start = ((), (), s32[]{:S(2)}) async-start(), calls=%async_computation.5 | async-start | bytes 4456448 | tf_op jit(solution)/shard_map/all_gather | solution.py:21
  8.0 311.0 %all-gather.6.cloned.1.call-start = ((), (), s32[]{:S(2)}) async-start(), calls=%async_computation.2 | async-start | bytes 2162688 | tf_op jit(solution)/shard_map/all_gather | solution.py:9
  8.7 402.9 %all-gather.8.cloned.1.call-start = ((), (), s32[]{:S(2)}) async-start(), calls=%async_computation.3 | async-start | bytes 4456448 | tf_op jit(solution)/shard_map/all_gather | solution.py:15
  9.3 508.2 %all-gather.14.cloned.1.call-start = ((), (), s32[]{:S(2)}) async-start(), calls=%async_computation.6 | async-start | bytes 2162688 | tf_op jit(solution)/shard_map/all_gather | solution.py:30
  417.4 102.0 %all-to-all-start = ((bf16[16,128,256]{1,2,0:T(8,128)(2,1)}), bf16[16,128,256]{1,2,0:T(8,128)(2,1)S(1)}, u32[]{:S(2)}, u32[]{:S(2)}) async-start(bf16[16,128,256]{1,2,0:T(8,128)(2,1)} %stack.2), calls=%async_computation | async-start | bytes 2097152 | tf_op jit(solution)/shard_map/all_to_all | solution.py:28
Sparse Core Ops, SparseCore 0:
  9.4 111.2 all-gather.9
  124.0 89.3 all-gather.11
  215.5 103.5 all-gather.5
  322.2 89.3 all-gather.7
  413.5 104.0 all-gather.13
